TPU v7x, 32 devices: a whole 2x2x4 slice. The times are simulated.
32 devices in a mesh: shard: 4 (over y, core), replica: 8 (over z, x).
Axes of the slice: x: 2, y: 2, z: 4, core: 2. Of those that a mesh axis runs over, the one named last changes fastest.
Arguments:
- tokens: bfloat16 [8, 1024, 1024], P('replica', 'shard'), may hold values from -6 to 6
- cotangent: bfloat16 [8, 1024, 1024], P('replica', 'shard'), may hold values from -6 to 6
- lengths: int32 [8], P('replica'), may hold values from 256 to 1024, as said below
- block_order: int32 [8, 8], P('replica'), may hold values from 0 to 7, as said below
- norm1_gain: bfloat16 [1024], P('shard'), may hold values from 0.099609375 to 1.8984375
- query_weight: bfloat16 [1024, 2048], P('shard'), may hold values from -0.1875 to 0.1875
- key_weight: bfloat16 [1024, 1024], P('shard'), may hold values from -0.1875 to 0.1875
- value_weight: bfloat16 [1024, 1024], P('shard'), may hold values from -0.1875 to 0.1875
- output_weight: bfloat16 [2048, 1024], P('shard'), may hold values from -1.5 to 1.5
- query_gain: bfloat16 [128], P('shard'), may hold values from 0.099609375 to 1.8984375
- key_gain: bfloat16 [128], P('shard'), may hold values from 0.099609375 to 1.8984375
- norm2_gain: bfloat16 [1024], P('shard'), may hold values from 0.099609375 to 1.8984375
- gate_weight: bfloat16 [1024, 3072], P('shard'), may hold values from -0.1875 to 0.1875
- up_weight: bfloat16 [1024, 3072], P('shard'), may hold values from -0.1875 to 0.1875
- down_weight: bfloat16 [3072, 1024], P('shard'), may hold values from -0.109375 to 0.109375
Outputs:
- output: bfloat16 [8, 1024, 1024], P('replica', 'shard')
- input_grad: float32 [8, 1024, 1024], P('replica', 'shard')
- norm1_gain_grad: float32 [1024], P('shard')
- query_weight_grad: float32 [1024, 2048], P('shard')
- key_weight_grad: float32 [1024, 1024], P('shard')
- value_weight_grad: float32 [1024, 1024], P('shard')
- output_weight_grad: float32 [2048, 1024], P('shard')
- query_gain_grad: float32 [128], P('shard')
- key_gain_grad: float32 [128], P('shard')
- norm2_gain_grad: float32 [1024], P('shard')
- gate_weight_grad: float32 [1024, 3072], P('shard')
- up_weight_grad: float32 [1024, 3072], P('shard')
- down_weight_grad: float32 [3072, 1024], P('shard')
Inputs may be any that keep to these rules, and one draw needn't show every extreme that they name: `lengths`: in every group of 1 sequence one has 1024 valid tokens; valid tokens hold positions 0 to length - 1. `block_order`: each row is a permutation of 0 to 7 in which places 2j and 2j + 1 hold blocks that add up to 7.
All inputs are finite; a program needn't handle non-finite values.
Results may differ from a plain program's by a relative error of at most 0.013.
Values may be sent and summed in bfloat16 or wider, within the bound.
A program may use at most 256 MiB of HBM per device.

v0:
```python
import jax
import jax.numpy as jnp
from jax import lax
from jax.sharding import PartitionSpec as P

EPSILON = 1e-06
ROPE_BASE = 1000000.0
BF = jnp.bfloat16
F32 = jnp.float32


def rms_scale(values, gain_vec):
    return (
        values * lax.rsqrt(jnp.mean(values * values, axis=-1, keepdims=True) + EPSILON) * gain_vec
    )


def rotate_half(values, cosine, sine_table):
    middle = values.shape[-1] // 2
    turned = jnp.concatenate([-values[..., middle:], values[..., :middle]], axis=-1)
    return values * cosine + turned * sine_table


def rotary_tables(position, head_width):
    middle = head_width // 2
    exponent = jnp.arange(middle, dtype=F32) * 2.0 / head_width
    inverse = ROPE_BASE ** (-exponent)
    phases = position.astype(F32)[..., None] * inverse
    phases = jnp.concatenate([phases, phases], axis=-1)
    return (jnp.cos(phases), jnp.sin(phases))


def mm(a, b):
    return jnp.einsum("ri,io->ro", a, b, preferred_element_type=F32)


def mm_t(a, b):
    return jnp.einsum("ro,io->ri", a, b, preferred_element_type=F32)


def mm_w(a, b):
    return jnp.einsum("ri,ro->io", a, b, preferred_element_type=F32)


def gather_rows(v):
    return lax.all_gather(v, "shard", axis=0, tiled=True)


def scatter_rows(v):
    return lax.psum_scatter(v.astype(BF), "shard", scatter_dimension=0, tiled=True).astype(F32)


def to_columns(w):
    return lax.all_to_all(w, "shard", split_axis=1, concat_axis=0, tiled=True)


def to_rows(g):
    return lax.all_to_all(g, "shard", split_axis=0, concat_axis=1, tiled=True)


def shards(
    tokens,
    cotangent,
    lengths,
    block_order,
    norm1_gain,
    query_weight,
    key_weight,
    value_weight,
    output_weight,
    query_gain,
    key_gain,
    norm2_gain,
    gate_weight,
    up_weight,
    down_weight,
):
    shard_count = lax.axis_size("shard")
    row_count = tokens.shape[1]
    block_count = block_order.shape[1]
    slot_len = row_count * shard_count
    block_len = slot_len // block_count
    head_width = query_gain.shape[0] * shard_count
    score_scale = head_width ** (-0.5)
    gains = lax.all_gather(
        jnp.concatenate([norm1_gain, norm2_gain, query_gain, key_gain]), "shard", axis=0
    )
    wide = norm1_gain.shape[0]
    gain_one = gains[:, :wide].reshape(-1).astype(F32)
    gain_two = gains[:, wide : 2 * wide].reshape(-1).astype(F32)
    gain_query = gains[:, 2 * wide : 2 * wide + query_gain.shape[0]].reshape(-1).astype(F32)
    gain_key = gains[:, 2 * wide + query_gain.shape[0] :].reshape(-1).astype(F32)
    w_qkv = tuple((to_columns(w) for w in (query_weight, key_weight, value_weight)))
    w_gate, w_up = (to_columns(gate_weight), to_columns(up_weight))
    heads = w_qkv[0].shape[1] // head_width
    kvs = w_qkv[1].shape[1] // head_width
    per = heads // kvs
    offsets = jnp.arange(slot_len, dtype=jnp.int32)
    pos_all = (
        jnp.repeat(block_order[0], block_len, total_repeat_length=slot_len) * block_len
        + offsets % block_len
    )
    pos_local = lax.dynamic_slice_in_dim(pos_all, lax.axis_index("shard") * row_count, row_count)
    valid_rows = (pos_local < lengths[0]).astype(F32)[:, None]
    allowed = pos_all[None, None, None, :] <= pos_all[None, None, :, None]
    inputs = tokens[0].astype(F32)
    normed_f, norm_one_back = jax.vjp(rms_scale, inputs, gain_one)
    normed = gather_rows(normed_f.astype(BF))
    grad_result = cotangent[0].astype(F32) * valid_rows
    grad_branch = gather_rows(grad_result.astype(BF))
    query_raw = mm(normed, w_qkv[0]).reshape(slot_len, heads, head_width)
    key_raw = mm(normed, w_qkv[1]).reshape(slot_len, kvs, head_width)
    value = mm(normed, w_qkv[2]).astype(BF).reshape(slot_len, kvs, head_width)
    cosine, sine = rotary_tables(pos_all, head_width)
    cosine, sine = (cosine[:, None, :], sine[:, None, :])

    def turn(q, k, gq, gk):
        return (
            rotate_half(rms_scale(q, gq), cosine, sine),
            rotate_half(rms_scale(k, gk), cosine, sine),
        )

    turned, turn_back = jax.vjp(turn, query_raw, key_raw, gain_query, gain_key)
    query = turned[0].astype(BF).reshape(slot_len, kvs, per, head_width)
    key = turned[1].astype(BF)

    def scores_of():
        raw = jnp.einsum("rkgd,tkd->kgrt", query, key, preferred_element_type=F32) * score_scale
        return jnp.where(allowed, raw, -1e30)

    scores = scores_of()
    row_top = jnp.max(scores, axis=-1, keepdims=True)
    log_total = row_top + jnp.log(jnp.sum(jnp.exp(scores - row_top), axis=-1, keepdims=True))
    probs = jnp.exp(scores - log_total).astype(BF)
    mixed = jnp.einsum("kgrt,tkd->rkgd", probs, value, preferred_element_type=F32)
    mixed = mixed.reshape(slot_len, heads * head_width).astype(BF)
    hidden = inputs + scatter_rows(mm(mixed, output_weight))
    normed2_f, norm_two_back = jax.vjp(rms_scale, hidden, gain_two)
    normed2 = gather_rows(normed2_f.astype(BF))
    active_f, swish_back = jax.vjp(
        lambda a, b: jax.nn.silu(a) * b, mm(normed2, w_gate), mm(normed2, w_up)
    )
    active = active_f.astype(BF)
    output = (valid_rows * (hidden + scatter_rows(mm(active, down_weight)))).astype(BF)
    grad_gate_f, grad_up_f = swish_back(mm_t(grad_branch, down_weight))
    grad_gate, grad_up = (grad_gate_f.astype(BF), grad_up_f.astype(BF))
    grad_hidden_norm, grad_gain_two = norm_two_back(
        scatter_rows(mm_t(grad_gate, w_gate) + mm_t(grad_up, w_up))
    )
    grad_hidden = grad_result + grad_hidden_norm
    grad_mixed_in = gather_rows(grad_hidden.astype(BF))
    grad_mixed = mm_t(grad_mixed_in, output_weight).astype(BF)
    grad_mixed = grad_mixed.reshape(slot_len, kvs, per, head_width)
    probs_f = jnp.exp(scores_of() - log_total)
    grad_probs = jnp.einsum("rkgd,tkd->kgrt", grad_mixed, value, preferred_element_type=F32)
    grad_value = jnp.einsum(
        "kgrt,rkgd->tkd", probs_f.astype(BF), grad_mixed, preferred_element_type=F32
    )
    row_inner = jnp.sum(probs_f * grad_probs, axis=-1, keepdims=True)
    grad_scores = (probs_f * (grad_probs - row_inner)).astype(BF)
    grad_query = (
        jnp.einsum("kgrt,tkd->rkgd", grad_scores, key, preferred_element_type=F32) * score_scale
    )
    grad_key = (
        jnp.einsum("kgrt,rkgd->tkd", grad_scores, query, preferred_element_type=F32) * score_scale
    )
    grad_query_raw, grad_key_raw, grad_gain_query, grad_gain_key = turn_back(
        (grad_query.reshape(slot_len, heads, head_width), grad_key)
    )
    grad_query_b = grad_query_raw.reshape(slot_len, -1).astype(BF)
    grad_key_b = grad_key_raw.reshape(slot_len, -1).astype(BF)
    grad_value_b = grad_value.reshape(slot_len, -1).astype(BF)
    grad_normed = (
        mm_t(grad_query_b, w_qkv[0]) + mm_t(grad_key_b, w_qkv[1]) + mm_t(grad_value_b, w_qkv[2])
    )
    grad_inputs_norm, grad_gain_one = norm_one_back(scatter_rows(grad_normed))
    input_grad = grad_hidden + grad_inputs_norm

    def total(v):
        return lax.psum(v.astype(BF), "replica").astype(F32)

    grad_down = total(mm_w(active, grad_branch))
    grad_gate_w = to_rows(total(mm_w(normed2, grad_gate)).astype(BF)).astype(F32)
    grad_up_w = to_rows(total(mm_w(normed2, grad_up)).astype(BF)).astype(F32)
    grad_output_w = total(mm_w(mixed, grad_mixed_in))
    grad_query_w = to_rows(total(mm_w(normed, grad_query_b)).astype(BF)).astype(F32)
    grad_key_w = to_rows(total(mm_w(normed, grad_key_b)).astype(BF)).astype(F32)
    grad_value_w = to_rows(total(mm_w(normed, grad_value_b)).astype(BF)).astype(F32)
    small = jnp.concatenate([grad_gain_one, grad_gain_two, grad_gain_query, grad_gain_key])
    small = lax.psum(small, ("shard", "replica"))
    at = lax.axis_index("shard")
    hw = query_gain.shape[0]

    def own(start, size):
        return lax.dynamic_slice_in_dim(small, start + at * size, size)

    model = wide * shard_count
    return (
        output[None],
        input_grad[None],
        own(0, wide),
        grad_query_w,
        grad_key_w,
        grad_value_w,
        grad_output_w,
        own(2 * model, hw),
        own(2 * model + head_width, hw),
        own(model, wide),
        grad_gate_w,
        grad_up_w,
        grad_down,
    )


def solution(mesh):
    rows, mat, vec = (P("replica", "shard", None), P("shard", None), P("shard"))
    placed = (rows, rows, P("replica"), P("replica", None), vec, mat, mat, mat, mat)
    placed += (vec, vec, vec, mat, mat, mat)
    outs = (rows, rows, vec, mat, mat, mat, mat, vec, vec, vec, mat, mat, mat)
    return jax.shard_map(shards, mesh=mesh, in_specs=placed, out_specs=outs, check_vma=False)
```

profile of v0, /device:TPU:0, one launch (start us, length us, event | category | flops | bytes accessed | tf_op | source)
XLA Modules:
  0.0 764.7 jit_solution(12287463658765484522)
XLA Ops:
  11.5 8.5 %all-reduce.4 = bf16[2304]{0:T(1024)(128)(2,1)S(1)} all-reduce(bf16[2304]{0:T(1024)(128)(2,1)S(1)} %dynamic-update-slice.3), channel_id=2, replica_groups=mesh['shard'=4,'replica'=8] {'shard'}, use_global_device_ids=true, to_apply=%add.4 | all-reduce | flops 2304 | bytes 9216
  28.5 4.6 compare_select_fusion.1
  33.1 6.2 all-to-all-done.1
  47.2 5.5 all-to-all-done
  64.9 6.6 all-to-all-done.2
  92.0 6.1 convolution_convert_fusion.8
  102.1 31.8 %reduce-scatter.5.cloned.1.call-done = bf16[256,1024]{1,0:T(8,128)(2,1)} async-done(((bf16[1024,1024]{1,0:T(8,128)(2,1)}), bf16[256,1024]{1,0:T(8,128)(2,1)}) %reduce-scatter.5.cloned.1.call-update) | async-done | bytes 524304 | tf_op jit(solution)/shard_map/reduce_scatter | solution.py:50
  149.6 25.8 %all-to-all-done.3 = bf16[256,4,768]{0,2,1:T(8,128)(2,1)} async-done(((bf16[256,4,768]{0,2,1:T(8,128)(2,1)}), bf16[256,4,768]{0,2,1:T(8,128)(2,1)}, u32[]{:S(2)}, u32[]{:S(2)}) %all-to-all-start.3) | async-done | bytes 1572896 | tf_op jit(solution)/shard_map/all_to_all | solution.py:54
  182.7 28.1 %all-to-all-done.4 = bf16[256,4,768]{0,2,1:T(8,128)(2,1)} async-done(((bf16[256,4,768]{0,2,1:T(8,128)(2,1)}), bf16[256,4,768]{0,2,1:T(8,128)(2,1)}, u32[]{:S(2)}, u32[]{:S(2)}) %all-to-all-start.4) | async-done | bytes 1572896 | tf_op jit(solution)/shard_map/all_to_all | solution.py:54
  213.4 5.6 fusion.63
  222.5 7.2 multiply_convert_fusion
  235.5 31.5 %reduce-scatter.9.cloned.1.call-done = bf16[256,1024]{1,0:T(8,128)(2,1)} async-done(((bf16[1024,1024]{1,0:T(8,128)(2,1)}), bf16[256,1024]{1,0:T(8,128)(2,1)}) %reduce-scatter.9.cloned.1.call-update) | async-done | bytes 524304 | tf_op jit(solution)/shard_map/reduce_scatter | solution.py:50
  271.8 5.2 convolution_convert_fusion.3
  283.1 11.0 %all-gather.12.cloned.1.call-done = bf16[1024,1024]{1,0:T(8,128)(2,1)} async-done(((bf16[256,1024]{1,0:T(8,128)(2,1)}), bf16[1024,1024]{1,0:T(8,128)(2,1)}) %all-gather.12.cloned.1.call-update) | async-done | bytes 2097168 | tf_op jit(solution)/shard_map/all_gather | solution.py:46
  297.2 8.5 %fusion.18 = bf16[2,128,1024]{2,1,0:T(8,128)(2,1)S(1)} fusion(bf16[1024,2,2,128]{0,3,2,1:T(8,128)(2,1)S(1)} %bitcast.261, f32[2,1024,1024,2]{2,1,3,0:T(8,128)} %copy-done.1, f32[2,2,1024]{2,1,0:T(2,128)S(1)} %log_add_fusion, pred[1024,1024]{0,1:T(8,128)(4,1)S(1)} %broadcast_compare_fusion), kind=kOutput, calls=%fused_computation.65 | convolution fusion | flops 1090781184 | bytes 19415040 | tf_op jit(solution)/shard_map/kgrt,rkgd->tkd/dot_general | solution.py:156
  305.8 12.4 %fusion = (f32[2,2,1024]{2,1,0:T(2,128)S(1)}, f32[2,1024,1024,2]{2,1,3,0:T(8,128)}) fusion(f32[2,1024,1024,2]{2,1,3,0:T(8,128)} %copy-done.1, f32[2,2,1024]{2,1,0:T(2,128)S(1)} %log_add_fusion, pred[1024,1024]{0,1:T(8,128)(4,1)S(1)} %broadcast_compare_fusion, bf16[1024,2,128,1]{0,2,3,1:T(8,128)(2,1)S(1)} %bitcast.264, bf16[1024,2,2,128]{0,3,2,1:T(8,128)(2,1)S(1)} %bitcast.262), kind=kOutput, calls=%fused_computation.2 | convolution fusion | flops 1094709248 | bytes 36208640 | tf_op jit(solution)/shard_map/rkgd,tkd->kgrt/dot_general | solution.py:155
  318.2 12.4 %fusion.2 = bf16[2,2,1024,1024]{2,3,1,0:T(8,128)(2,1)S(1)} fusion(f32[2,1024,1024,2]{2,1,3,0:T(8,128)} %get-tuple-element.84, f32[2,1024,1024,2]{2,1,3,0:T(8,128)} %copy-done.1, f32[2,2,1024]{2,1,0:T(2,128)S(1)} %get-tuple-element.83, f32[2,2,1024]{2,1,0:T(2,128)S(1)} %log_add_fusion, pred[1024,1024]{0,1:T(8,128)(4,1)S(1)} %broadcast_compare_fusion), kind=kLoop, calls=%fused_computation.4 | loop fusion | flops 25165824 | bytes 43024384 | tf_op jit(solution)/shard_map/convert_element_type | solution.py:160
  363.1 247.1 %all-reduce.8.cloned.1.call-done = (bf16[4,256,512]{2,1,0:T(8,128)(2,1)}, bf16[4,256,256]{2,1,0:T(8,128)(2,1)}, bf16[4,256,256]{2,1,0:T(8,128)(2,1)}, bf16[512,1...) async-done(((bf16[4,256,512]{2,1,0:T(8,128)(2,1)}, bf16[4,256,256]{2,1,0:T(8,128)(2,1)}, ...) | async-done | bytes 7864336 | tf_op jit(solution)/shard_map/psum | solution.py:180
  610.2 13.2 %all_to_all.160 = bf16[4,256,256]{2,1,0:T(8,128)(2,1)} all-to-all(bf16[4,256,256]{2,1,0:T(8,128)(2,1)} %get-tuple-element.34), channel_id=1, replica_groups=mesh['shard'=4,'replica'=8] {'shard'}, dimensions={0} | all-to-all | bytes 1048576 | tf_op jit(solution)/shard_map/all_to_all | solution.py:58
  623.4 18.6 %all_to_all.161 = bf16[4,256,256]{2,1,0:T(8,128)(2,1)} all-to-all(bf16[4,256,256]{2,1,0:T(8,128)(2,1)} %get-tuple-element.35), channel_id=1, replica_groups=mesh['shard'=4,'replica'=8] {'shard'}, dimensions={0} | all-to-all | bytes 1048576 | tf_op jit(solution)/shard_map/all_to_all | solution.py:58
  642.0 17.6 %all_to_all.162 = bf16[4,256,512]{2,1,0:T(8,128)(2,1)} all-to-all(bf16[4,256,512]{2,1,0:T(8,128)(2,1)S(1)} %copy-done.34), channel_id=1, replica_groups=mesh['shard'=4,'replica'=8] {'shard'}, dimensions={0} | all-to-all | bytes 2097152 | tf_op jit(solution)/shard_map/all_to_all | solution.py:58
  659.6 4.5 all-to-all-start.9
  665.7 62.1 %psum.56 = f32[2304]{0:T(1024)S(1)} all-reduce(f32[2304]{0:T(1024)S(1)} %pad_maximum_fusion.1), channel_id=1, replica_groups=mesh['shard'=4,'replica'=8] {'shard','replica'}, use_global_device_ids=true, to_apply=%region_19.20 | all-reduce | flops 2304 | bytes 18432 | tf_op jit(solution)/shard_map/psum | solution.py:190
  749.1 6.4 all-to-all-done.8
  (239 shorter events, 161.8 us)
Async XLA Ops:
  7.2 215.3 %copy-start = (bf16[768,1024]{1,0:T(8,128)(2,1)S(1)}, bf16[768,1024]{1,0:T(8,128)(2,1)}, u32[]{:S(2)}) copy-start(bf16[768,1024]{1,0:T(8,128)(2,1)} %param.31) | copy-start | bytes 4718596
  7.2 15.0 %copy-start.39 = (bf16[256,1024]{1,0:T(8,128)(2,1)S(1)}, bf16[256,1024]{1,0:T(8,128)(2,1)}, u32[]{:S(2)}) copy-start(bf16[256,1024]{1,0:T(8,128)(2,1)} %param.23) | copy-start | bytes 1572868
  7.2 66.6 %all-gather.6.cloned.1.call-start = ((), (), s32[]{:S(2)}) async-start(), calls=%async_computation.14 | async-start | bytes 2621440 | tf_op jit(solution)/shard_map/all_gather | solution.py:46
  23.4 15.9 %all-to-all-start.1 = ((bf16[256,4,256]{2,0,1:T(8,128)(2,1)}), bf16[256,4,256]{2,0,1:T(8,128)(2,1)S(1)}, u32[]{:S(2)}, u32[]{:S(2)}) async-start(bf16[256,4,256]{2,0,1:T(8,128)(2,1)} %copy.103), calls=%async_computation.1 | async-start | bytes 1048576 | tf_op jit(solution)/shard_map/all_to_all | solution.py:54
  39.3 13.4 %all-to-all-start = ((bf16[256,4,256]{0,2,1:T(8,128)(2,1)}), bf16[256,4,256]{0,2,1:T(8,128)(2,1)}, u32[]{:S(2)}, u32[]{:S(2)}) async-start(bf16[256,4,256]{0,2,1:T(8,128)(2,1)} %bitcast.17), calls=%async_computation | async-start | bytes 1048576 | tf_op jit(solution)/shard_map/all_to_all | solution.py:54
  52.7 18.8 %all-to-all-start.2 = ((bf16[256,4,512]{2,0,1:T(8,128)(2,1)}), bf16[256,4,512]{2,0,1:T(8,128)(2,1)}, u32[]{:S(2)}, u32[]{:S(2)}) async-start(bf16[256,4,512]{2,0,1:T(8,128)(2,1)} %copy.106), calls=%async_computation.2 | async-start | bytes 2097152 | tf_op jit(solution)/shard_map/all_to_all | solution.py:54
  57.0 76.9 %reduce-scatter.5.cloned.1.call-start = ((), (), s32[]{:S(2)}) async-start(), calls=%async_computation.15 | async-start | bytes 2621440 | tf_op jit(solution)/shard_map/reduce_scatter | solution.py:50
  60.2 21.9 %copy-start.8 = (f32[1024,128]{0,1:T(8,128)}, f32[1024,128]{0,1:T(8,128)S(1)}, u32[]{:S(2)}) copy-start(f32[1024,128]{0,1:T(8,128)S(1)} %get-tuple-element.60) | copy-start | bytes 1572868
  102.0 31.9 %copy-start.4 = (bf16[1,256,1024]{2,1,0:T(8,128)(2,1)S(1)}, bf16[1,256,1024]{2,1,0:T(8,128)(2,1)}, u32[]{:S(2)}) copy-start(bf16[1,256,1024]{2,1,0:T(8,128)(2,1)} %param.17) | copy-start | bytes 1572868
  102.0 111.4 %all-gather.8.cloned.1.call-start = ((), (), s32[]{:S(2)}) async-start(), calls=%async_computation.16 | async-start | bytes 2621440 | tf_op jit(solution)/shard_map/all_gather | solution.py:46
  139.8 35.6 %all-to-all-start.3 = ((bf16[256,4,768]{0,2,1:T(8,128)(2,1)}), bf16[256,4,768]{0,2,1:T(8,128)(2,1)}, u32[]{:S(2)}, u32[]{:S(2)}) async-start(bf16[256,4,768]{0,2,1:T(8,128)(2,1)} %bitcast.234), calls=%async_computation.4 | async-start | bytes 3145728 | tf_op jit(solution)/shard_map/all_to_all | solution.py:54
  144.2 78.3 %all-gather.10.cloned.1.call-start = ((), (), s32[]{:S(2)}) async-start(), calls=%async_computation.18 | async-start | bytes 2621440 | tf_op jit(solution)/shard_map/all_gather | solution.py:46
  175.4 35.4 %all-to-all-start.4 = ((bf16[256,4,768]{0,2,1:T(8,128)(2,1)}), bf16[256,4,768]{0,2,1:T(8,128)(2,1)}, u32[]{:S(2)}, u32[]{:S(2)}) async-start(bf16[256,4,768]{0,2,1:T(8,128)(2,1)} %bitcast.235), calls=%async_computation.5 | async-start | bytes 3145728 | tf_op jit(solution)/shard_map/all_to_all | solution.py:54
  179.8 87.2 %reduce-scatter.9.cloned.1.call-start = ((), (), s32[]{:S(2)}) async-start(), calls=%async_computation.19 | async-start | bytes 2621440 | tf_op jit(solution)/shard_map/reduce_scatter | solution.py:50
  235.4 58.6 %all-gather.12.cloned.1.call-start = ((), (), s32[]{:S(2)}) async-start(), calls=%async_computation.20 | async-start | bytes 2621440 | tf_op jit(solution)/shard_map/all_gather | solution.py:46
  271.3 338.9 %all-reduce.8.cloned.1.call-start = ((), (), s32[]{:S(2)}) async-start(), calls=%async_computation.22 | async-start | bytes 15728640 | tf_op jit(solution)/shard_map/psum | solution.py:180
  305.8 39.2 %copy-start.38 = (bf16[2,128,1024]{2,1,0:T(8,128)(2,1)}, bf16[2,128,1024]{2,1,0:T(8,128)(2,1)S(1)}, u32[]{:S(2)}) copy-start(bf16[2,128,1024]{2,1,0:T(8,128)(2,1)S(1)} %fusion.18) | copy-start | bytes 1572868
  350.4 313.7 %reduce-scatter.11.cloned.1.call-start = ((), (), s32[]{:S(2)}) async-start(), calls=%async_computation.21 | async-start | bytes 2621440 | tf_op jit(solution)/shard_map/reduce_scatter | solution.py:50
  358.5 370.0 %reduce-scatter.7.cloned.1.call-start = ((), (), s32[]{:S(2)}) async-start(), calls=%async_computation.17 | async-start | bytes 2621440 | tf_op jit(solution)/shard_map/reduce_scatter | solution.py:50
  610.2 31.7 %copy-start.34 = (bf16[4,256,512]{2,1,0:T(8,128)(2,1)S(1)}, bf16[4,256,512]{2,1,0:T(8,128)(2,1)}, u32[]{:S(2)}) copy-start(bf16[4,256,512]{2,1,0:T(8,128)(2,1)} %get-tuple-element.33) | copy-start | bytes 3145732
  659.6 68.9 %copy-start.7 = (bf16[256,1024]{1,0:T(8,128)(2,1)S(1)}, bf16[256,1024]{1,0:T(8,128)(2,1)}, u32[]{:S(2)}) copy-start(bf16[256,1024]{1,0:T(8,128)(2,1)} %reduce-scatter.5.cloned.1.call-done) | copy-start | bytes 1572868
  659.6 68.9 %copy-start.12 = (bf16[1,256,1024]{2,1,0:T(8,128)(2,1)S(1)}, bf16[1,256,1024]{2,1,0:T(8,128)(2,1)}, u32[]{:S(2)}) copy-start(bf16[1,256,1024]{2,1,0:T(8,128)(2,1)} %param.18) | copy-start | bytes 1572868
  659.6 72.2 %all-to-all-start.9 = ((bf16[4,256,768]{2,1,0:T(8,128)(2,1)}), bf16[4,256,768]{2,1,0:T(8,128)(2,1)}, u32[]{:S(2)}, u32[]{:S(2)}) async-start(bf16[4,256,768]{2,1,0:T(8,128)(2,1)} %get-tuple-element.38), calls=%async_computation.13 | async-start | bytes 3145728 | tf_op jit(solution)/shard_map/all_to_all | solution.py:58
  731.9 23.7 %all-to-all-start.8 = ((bf16[4,256,768]{2,1,0:T(8,128)(2,1)}), bf16[4,256,768]{2,1,0:T(8,128)(2,1)S(1)}, u32[]{:S(2)}, u32[]{:S(2)}) async-start(bf16[4,256,768]{2,1,0:T(8,128)(2,1)} %get-tuple-element.37), calls=%async_computation.12 | async-start | bytes 3145728 | tf_op jit(solution)/shard_map/all_to_all | solution.py:58
  (46 other events, 160.9 us)
Sparse Core Ops, SparseCore 0:
  22.3 26.2 all-gather.5
  102.1 31.7 reduce-scatter.4
  137.4 33.7 all-gather.7
  172.7 33.7 all-gather.9
  235.6 31.4 reduce-scatter.8
  271.5 22.5 all-gather.11
  350.6 259.6 all-reduce.7
  613.3 35.3 reduce-scatter.10
  652.0 42.2 reduce-scatter.6
where the time goes:
time: 769 us; the launch traced here: 765 us
  waiting for transfers between devices  400 us (52%)
  blocking collectives  120 us (16%)
  matrix products  97.4 us (13%)
  other arithmetic  56.2 us (7%)
  local copies, waits for them, and re-layouts  44.7 us (6%)
  starting transfers between devices  29.9 us (4%)
  between operations  16.3 us (2%)
    psum x1, waiting for transfers between devices, total(): return lax.psum(v.astype(BF), 'replica').astype(F32)  247 us
    all_to_all x5, waiting for transfers between devices, to_columns(): return lax.all_to_all(w, 'shard', split_axis=1, concat_axis=0, tiled=True)  72.1 us
    reduce_scatter x4, waiting for transfers between devices, scatter_rows(): lax.psum_scatter(v.astype(BF), 'shard', scatter_dimension=0, tiled=True)  63.4 us
    psum x1, blocking collectives, shards(): small = lax.psum(small, ('shard', 'replica'))  62.1 us
    all_to_all x3, blocking collectives, to_rows(): return lax.all_to_all(g, 'shard', split_axis=0, concat_axis=1, tiled=True)  49.4 us
    dot_general x7, matrix products, mm(): return jnp.einsum('ri,io->ro', a, b, preferred_element_type=F32)  22 us
    dot_general x7, matrix products, mm_t(): return jnp.einsum('ro,io->ri', a, b, preferred_element_type=F32)  21.9 us
    all_to_all x5, starting transfers between devices, to_columns(): return lax.all_to_all(w, 'shard', split_axis=1, concat_axis=0, tiled=True)  20.6 us
  transfers between devices with their start and end apart: 16, of which 10 were waited for; matrix products, arithmetic and copies ran while one was open for 11% of the time, Pallas kernels for 0%

commit v1 on v0

--- a/solution.py
+++ b/solution.py
@@ -55,7 +55,16 @@
 
 
 def to_rows(g):
-    return lax.all_to_all(g, "shard", split_axis=0, concat_axis=1, tiled=True)
+    sites_solve = lambda array_here: jnp.concatenate(
+        lax.all_to_all(
+            jnp.stack(jnp.split(array_here, lax.axis_size("shard"), 0)),
+            "shard",
+            split_axis=0,
+            concat_axis=0,
+        ),
+        1,
+    )
+    return sites_solve(g)
 
 
 def shards(

time: 769 us -> 797 us (1.036)
  blocking collectives: 120 us -> 68.8 us
  local copies, waits for them, and re-layouts: 44.7 us -> 70.8 us
  waiting for transfers between devices: 400 us -> 424 us
  other arithmetic: 56.2 us -> 72.5 us
  starting transfers between devices: 29.9 us -> 42.1 us
    all_to_all x3 -> x0, blocking collectives: 49.4 us -> none  [to_rows(): return lax.all_to_all(g, 'shard', split_axis=0, concat_axis=1, tiled=True)]
    all_to_all x2 -> x5, waiting for transfers between devices: 6.45 us -> 30.2 us  [to_rows(): lax.all_to_all(jnp.stack(jnp.split(array_here, lax.axis_size('shard'), 0)...]
    unnamed x118 -> x141, local copies, waits for them, and re-layouts: 20.5 us -> 35 us
    all_to_all x2 -> x5, starting transfers between devices: 8.1 us -> 20.3 us  [to_rows(): lax.all_to_all(jnp.stack(jnp.split(array_here, lax.axis_size('shard'), 0)...]
    convert_element_type x0 -> x5, other arithmetic: none -> 9.67 us  [the longest x1 3.34 us: shards(): to_rows(total(mm_w(normed2, grad_gate)).astype(BF)).astype(F32)]
  transfers between devices with their start and end apart: 16 -> 19, of which waited for: 10 -> 12; matrix products, arithmetic and copies ran while one was open for 11% -> 15% of each run, Pallas kernels for 0% -> 0%
where the time goes in v1:
time: 797 us; the launch traced here: 792 us
  waiting for transfers between devices  424 us (53%)
  matrix products  97.5 us (12%)
  other arithmetic  72.5 us (9%)
  local copies, waits for them, and re-layouts  70.8 us (9%)
  blocking collectives  68.8 us (9%)
  starting transfers between devices  42.1 us (5%)
  between operations  16.4 us (2%)
    psum x1, waiting for transfers between devices, total(): return lax.psum(v.astype(BF), 'replica').astype(F32)  247 us
    all_to_all x5, waiting for transfers between devices, to_columns(): return lax.all_to_all(w, 'shard', split_axis=1, concat_axis=0, tiled=True)  72.2 us
    reduce_scatter x4, waiting for transfers between devices, scatter_rows(): lax.psum_scatter(v.astype(BF), 'shard', scatter_dimension=0, tiled=True)  63.4 us
    psum x1, blocking collectives, shards(): small = lax.psum(small, ('shard', 'replica'))  60.3 us
    unnamed x141, local copies, waits for them, and re-layouts  35 us
    all_to_all x5, waiting for transfers between devices, to_rows(): lax.all_to_all(jnp.stack(jnp.split(array_here, lax.axis_size('shard'), 0)...  30.2 us
    dot_general x7, matrix products, mm(): return jnp.einsum('ri,io->ro', a, b, preferred_element_type=F32)  22 us
    dot_general x7, matrix products, mm_t(): return jnp.einsum('ro,io->ri', a, b, preferred_element_type=F32)  21.9 us
  transfers between devices with their start and end apart: 19, of which 12 were waited for; matrix products, arithmetic and copies ran while one was open for 15% of the time, Pallas kernels for 0%

profile of v1, /device:TPU:0, one launch (start us, length us, event | category | flops | bytes accessed | tf_op | source)
XLA Modules:
  0.0 792.2 jit_solution(4842083265763630549)
XLA Ops:
  11.6 8.5 %all-reduce.4 = bf16[2304]{0:T(1024)(128)(2,1)S(1)} all-reduce(bf16[2304]{0:T(1024)(128)(2,1)S(1)} %dynamic-update-slice.3), channel_id=2, replica_groups=mesh['shard'=4,'replica'=8] {'shard'}, use_global_device_ids=true, to_apply=%add.4 | all-reduce | flops 2304 | bytes 9216
  28.6 4.6 compare_select_fusion.1
  33.2 6.2 all-to-all-done.1
  47.3 5.5 all-to-all-done
  64.9 6.6 all-to-all-done.2
  92.1 6.1 convolution_convert_fusion.8
  102.1 31.8 %reduce-scatter.5.cloned.1.call-done = bf16[256,1024]{1,0:T(8,128)(2,1)} async-done(((bf16[1024,1024]{1,0:T(8,128)(2,1)}), bf16[256,1024]{1,0:T(8,128)(2,1)}) %reduce-scatter.5.cloned.1.call-update) | async-done | bytes 524304 | tf_op jit(solution)/shard_map/reduce_scatter | solution.py:50
  149.7 25.8 %all-to-all-done.3 = bf16[256,4,768]{0,2,1:T(8,128)(2,1)} async-done(((bf16[256,4,768]{0,2,1:T(8,128)(2,1)}), bf16[256,4,768]{0,2,1:T(8,128)(2,1)}, u32[]{:S(2)}, u32[]{:S(2)}) %all-to-all-start.3) | async-done | bytes 1572896 | tf_op jit(solution)/shard_map/all_to_all | solution.py:54
  182.8 28.1 %all-to-all-done.4 = bf16[256,4,768]{0,2,1:T(8,128)(2,1)} async-done(((bf16[256,4,768]{0,2,1:T(8,128)(2,1)}), bf16[256,4,768]{0,2,1:T(8,128)(2,1)}, u32[]{:S(2)}, u32[]{:S(2)}) %all-to-all-start.4) | async-done | bytes 1572896 | tf_op jit(solution)/shard_map/all_to_all | solution.py:54
  213.4 5.6 fusion.63
  222.5 7.3 multiply_convert_fusion
  235.6 31.5 %reduce-scatter.9.cloned.1.call-done = bf16[256,1024]{1,0:T(8,128)(2,1)} async-done(((bf16[1024,1024]{1,0:T(8,128)(2,1)}), bf16[256,1024]{1,0:T(8,128)(2,1)}) %reduce-scatter.9.cloned.1.call-update) | async-done | bytes 524304 | tf_op jit(solution)/shard_map/reduce_scatter | solution.py:50
  272.5 5.2 convolution_convert_fusion.3
  283.8 11.0 %all-gather.12.cloned.1.call-done = bf16[1024,1024]{1,0:T(8,128)(2,1)} async-done(((bf16[256,1024]{1,0:T(8,128)(2,1)}), bf16[1024,1024]{1,0:T(8,128)(2,1)}) %all-gather.12.cloned.1.call-update) | async-done | bytes 2097168 | tf_op jit(solution)/shard_map/all_gather | solution.py:46
  297.9 8.5 %fusion.18 = bf16[2,128,1024]{2,1,0:T(8,128)(2,1)S(1)} fusion(bf16[1024,2,2,128]{0,3,2,1:T(8,128)(2,1)S(1)} %bitcast.288, f32[2,1024,1024,2]{2,1,3,0:T(8,128)} %copy-done.1, f32[2,2,1024]{2,1,0:T(2,128)S(1)} %log_add_fusion, pred[1024,1024]{0,1:T(8,128)(4,1)S(1)} %broadcast_compare_fusion), kind=kOutput, calls=%fused_computation.67 | convolution fusion | flops 1090781184 | bytes 19415040 | tf_op jit(solution)/shard_map/kgrt,rkgd->tkd/dot_general | solution.py:165
  306.5 12.5 %fusion = (f32[2,2,1024]{2,1,0:T(2,128)S(1)}, f32[2,1024,1024,2]{2,1,3,0:T(8,128)}) fusion(f32[2,1024,1024,2]{2,1,3,0:T(8,128)} %copy-done.1, f32[2,2,1024]{2,1,0:T(2,128)S(1)} %log_add_fusion, pred[1024,1024]{0,1:T(8,128)(4,1)S(1)} %broadcast_compare_fusion, bf16[1024,2,128,1]{0,2,3,1:T(8,128)(2,1)S(1)} %bitcast.291, bf16[1024,2,2,128]{0,3,2,1:T(8,128)(2,1)S(1)} %bitcast.289), kind=kOutput, calls=%fused_computation.2 | convolution fusion | flops 1094709248 | bytes 36208640 | tf_op jit(solution)/shard_map/rkgd,tkd->kgrt/dot_general | solution.py:164
  318.9 12.4 %fusion.2 = bf16[2,2,1024,1024]{2,3,1,0:T(8,128)(2,1)S(1)} fusion(f32[2,1024,1024,2]{2,1,3,0:T(8,128)} %get-tuple-element.156, f32[2,1024,1024,2]{2,1,3,0:T(8,128)} %copy-done.1, f32[2,2,1024]{2,1,0:T(2,128)S(1)} %get-tuple-element.155, f32[2,2,1024]{2,1,0:T(2,128)S(1)} %log_add_fusion, pred[1024,1024]{0,1:T(8,128)(4,1)S(1)} %broadcast_compare_fusion), kind=kLoop, calls=%fused_computation.4 | loop fusion | flops 25165824 | bytes 43024384 | tf_op jit(solution)/shard_map/convert_element_type | solution.py:169
  359.7 4.5 convolution_convert_fusion.1
  364.2 247.1 %all-reduce.8.cloned.1.call-done = (bf16[1024,512]{1,0:T(8,128)(2,1)}, bf16[1024,256]{1,0:T(8,128)(2,1)}, bf16[1024,256]{1,0:T(8,128)(2,1)}, bf16[512,1024]{1,0:...) async-done(((bf16[1024,512]{1,0:T(8,128)(2,1)}, bf16[1024,256]{1,0:T(8,128)(2,1)}, bf16[1024,256]{1,0:T(8,128)(2,1)}, ...) | async-done | bytes 7864336 | tf_op jit(solution)/shard_map/psum | solution.py:189
  617.9 7.9 %all-to-all-done.7 = bf16[4,256,256]{2,1,0:T(8,128)(2,1)S(1)} async-done(((bf16[4,256,256]{2,1,0:T(8,128)(2,1)}), bf16[4,256,256]{2,1,0:T(8,128)(2,1)S(1)}, u32[]{:S(2)}, u32[]{:S(2)}) %all-to-all-start.7) | async-done | bytes 524320 | tf_op jit(solution)/shard_map/all_to_all | solution.py:59
  631.8 12.0 %all-to-all-done.6 = bf16[4,256,256]{2,1,0:T(8,128)(2,1)S(1)} async-done(((bf16[4,256,256]{2,1,0:T(8,128)(2,1)}), bf16[4,256,256]{2,1,0:T(8,128)(2,1)S(1)}, u32[]{:S(2)}, u32[]{:S(2)}) %all-to-all-start.6) | async-done | bytes 524320 | tf_op jit(solution)/shard_map/all_to_all | solution.py:59
  652.4 10.2 %all-to-all-done.5 = bf16[4,256,512]{2,1,0:T(8,128)(2,1)} async-done(((bf16[4,256,512]{2,1,0:T(8,128)(2,1)}), bf16[4,256,512]{2,1,0:T(8,128)(2,1)}, u32[]{:S(2)}, u32[]{:S(2)}) %all-to-all-start.5) | async-done | bytes 1048608 | tf_op jit(solution)/shard_map/all_to_all | solution.py:59
  670.4 60.3 %psum.56 = f32[2304]{0:T(1024)} all-reduce(f32[2304]{0:T(1024)} %pad_maximum_fusion.6), channel_id=1, replica_groups=mesh['shard'=4,'replica'=8] {'shard','replica'}, use_global_device_ids=true, to_apply=%region_19.20 | all-reduce | flops 2304 | bytes 18432 | tf_op jit(solution)/shard_map/psum | solution.py:199
  738.2 4.8 all-to-all-start.8
  (273 shorter events, 211.7 us)
Async XLA Ops:
  7.2 215.4 %copy-start = (bf16[768,1024]{1,0:T(8,128)(2,1)S(1)}, bf16[768,1024]{1,0:T(8,128)(2,1)}, u32[]{:S(2)}) copy-start(bf16[768,1024]{1,0:T(8,128)(2,1)} %param.31) | copy-start | bytes 4718596
  7.2 66.6 %all-gather.6.cloned.1.call-start = ((), (), s32[]{:S(2)}) async-start(), calls=%async_computation.14 | async-start | bytes 2621440 | tf_op jit(solution)/shard_map/all_gather | solution.py:46
  23.5 15.9 %all-to-all-start.1 = ((bf16[256,4,256]{2,0,1:T(8,128)(2,1)}), bf16[256,4,256]{2,0,1:T(8,128)(2,1)S(1)}, u32[]{:S(2)}, u32[]{:S(2)}) async-start(bf16[256,4,256]{2,0,1:T(8,128)(2,1)} %copy.113), calls=%async_computation.1 | async-start | bytes 1048576 | tf_op jit(solution)/shard_map/all_to_all | solution.py:54
  39.4 13.4 %all-to-all-start = ((bf16[256,4,256]{0,2,1:T(8,128)(2,1)}), bf16[256,4,256]{0,2,1:T(8,128)(2,1)}, u32[]{:S(2)}, u32[]{:S(2)}) async-start(bf16[256,4,256]{0,2,1:T(8,128)(2,1)} %bitcast.17), calls=%async_computation | async-start | bytes 1048576 | tf_op jit(solution)/shard_map/all_to_all | solution.py:54
  52.7 18.8 %all-to-all-start.2 = ((bf16[256,4,512]{2,0,1:T(8,128)(2,1)}), bf16[256,4,512]{2,0,1:T(8,128)(2,1)}, u32[]{:S(2)}, u32[]{:S(2)}) async-start(bf16[256,4,512]{2,0,1:T(8,128)(2,1)} %copy.116), calls=%async_computation.2 | async-start | bytes 2097152 | tf_op jit(solution)/shard_map/all_to_all | solution.py:54
  57.0 77.0 %reduce-scatter.5.cloned.1.call-start = ((), (), s32[]{:S(2)}) async-start(), calls=%async_computation.15 | async-start | bytes 2621440 | tf_op jit(solution)/shard_map/reduce_scatter | solution.py:50
  102.1 31.9 %copy-start.4 = (bf16[1,256,1024]{2,1,0:T(8,128)(2,1)S(1)}, bf16[1,256,1024]{2,1,0:T(8,128)(2,1)}, u32[]{:S(2)}) copy-start(bf16[1,256,1024]{2,1,0:T(8,128)(2,1)} %param.17) | copy-start | bytes 1572868
  102.1 111.3 %all-gather.8.cloned.1.call-start = ((), (), s32[]{:S(2)}) async-start(), calls=%async_computation.16 | async-start | bytes 2621440 | tf_op jit(solution)/shard_map/all_gather | solution.py:46
  139.9 35.6 %all-to-all-start.3 = ((bf16[256,4,768]{0,2,1:T(8,128)(2,1)}), bf16[256,4,768]{0,2,1:T(8,128)(2,1)}, u32[]{:S(2)}, u32[]{:S(2)}) async-start(bf16[256,4,768]{0,2,1:T(8,128)(2,1)} %bitcast.267), calls=%async_computation.4 | async-start | bytes 3145728 | tf_op jit(solution)/shard_map/all_to_all | solution.py:54
  144.3 78.3 %all-gather.10.cloned.1.call-start = ((), (), s32[]{:S(2)}) async-start(), calls=%async_computation.18 | async-start | bytes 2621440 | tf_op jit(solution)/shard_map/all_gather | solution.py:46
  175.5 35.3 %all-to-all-start.4 = ((bf16[256,4,768]{0,2,1:T(8,128)(2,1)}), bf16[256,4,768]{0,2,1:T(8,128)(2,1)}, u32[]{:S(2)}, u32[]{:S(2)}) async-start(bf16[256,4,768]{0,2,1:T(8,128)(2,1)} %bitcast.268), calls=%async_computation.5 | async-start | bytes 3145728 | tf_op jit(solution)/shard_map/all_to_all | solution.py:54
  179.9 87.3 %reduce-scatter.9.cloned.1.call-start = ((), (), s32[]{:S(2)}) async-start(), calls=%async_computation.19 | async-start | bytes 2621440 | tf_op jit(solution)/shard_map/reduce_scatter | solution.py:50
  235.5 59.2 %all-gather.12.cloned.1.call-start = ((), (), s32[]{:S(2)}) async-start(), calls=%async_computation.20 | async-start | bytes 2621440 | tf_op jit(solution)/shard_map/all_gather | solution.py:46
  272.0 339.3 %all-reduce.8.cloned.1.call-start = ((), (), s32[]{:S(2)}) async-start(), calls=%async_computation.22 | async-start | bytes 15728640 | tf_op jit(solution)/shard_map/psum | solution.py:189
  306.4 39.7 %copy-start.42 = (bf16[2,128,1024]{2,1,0:T(8,128)(2,1)}, bf16[2,128,1024]{2,1,0:T(8,128)(2,1)S(1)}, u32[]{:S(2)}) copy-start(bf16[2,128,1024]{2,1,0:T(8,128)(2,1)S(1)} %fusion.18) | copy-start | bytes 1572868
  351.6 315.4 %reduce-scatter.11.cloned.1.call-start = ((), (), s32[]{:S(2)}) async-start(), calls=%async_computation.21 | async-start | bytes 2621440 | tf_op jit(solution)/shard_map/reduce_scatter | solution.py:50
  359.6 373.7 %reduce-scatter.7.cloned.1.call-start = ((), (), s32[]{:S(2)}) async-start(), calls=%async_computation.17 | async-start | bytes 2621440 | tf_op jit(solution)/shard_map/reduce_scatter | solution.py:50
  613.6 12.3 %all-to-all-start.7 = ((bf16[4,256,256]{2,1,0:T(8,128)(2,1)}), bf16[4,256,256]{2,1,0:T(8,128)(2,1)S(1)}, u32[]{:S(2)}, u32[]{:S(2)}) async-start(bf16[4,256,256]{2,1,0:T(8,128)(2,1)} %pad_maximum_fusion.5), calls=%async_computation.11 | async-start | bytes 1048576 | tf_op jit(solution)/shard_map/all_to_all | solution.py:59
  625.9 17.9 %all-to-all-start.6 = ((bf16[4,256,256]{2,1,0:T(8,128)(2,1)}), bf16[4,256,256]{2,1,0:T(8,128)(2,1)S(1)}, u32[]{:S(2)}, u32[]{:S(2)}) async-start(bf16[4,256,256]{2,1,0:T(8,128)(2,1)} %pad_maximum_fusion.4), calls=%async_computation.10 | async-start | bytes 1048576 | tf_op jit(solution)/shard_map/all_to_all | solution.py:59
  643.8 18.8 %all-to-all-start.5 = ((bf16[4,256,512]{2,1,0:T(8,128)(2,1)}), bf16[4,256,512]{2,1,0:T(8,128)(2,1)}, u32[]{:S(2)}, u32[]{:S(2)}) async-start(bf16[4,256,512]{2,1,0:T(8,128)(2,1)} %pad_maximum_fusion.2), calls=%async_computation.9 | async-start | bytes 2097152 | tf_op jit(solution)/shard_map/all_to_all | solution.py:59
  652.4 80.9 %copy-start.7 = (bf16[256,1024]{1,0:T(8,128)(2,1)S(1)}, bf16[256,1024]{1,0:T(8,128)(2,1)}, u32[]{:S(2)}) copy-start(bf16[256,1024]{1,0:T(8,128)(2,1)} %reduce-scatter.5.cloned.1.call-done) | copy-start | bytes 1572868
  652.4 80.9 %copy-start.12 = (bf16[1,256,1024]{2,1,0:T(8,128)(2,1)S(1)}, bf16[1,256,1024]{2,1,0:T(8,128)(2,1)}, u32[]{:S(2)}) copy-start(bf16[1,256,1024]{2,1,0:T(8,128)(2,1)} %param.18) | copy-start | bytes 1572868
  662.6 75.6 %all-to-all-start.9 = ((bf16[4,256,768]{2,1,0:T(8,128)(2,1)}), bf16[4,256,768]{2,1,0:T(8,128)(2,1)}, u32[]{:S(2)}, u32[]{:S(2)}) async-start(bf16[4,256,768]{2,1,0:T(8,128)(2,1)} %pad_maximum_fusion.1), calls=%async_computation.13 | async-start | bytes 3145728 | tf_op jit(solution)/shard_map/all_to_all | solution.py:59
  738.2 36.7 %all-to-all-start.8 = ((bf16[4,256,768]{2,1,0:T(8,128)(2,1)}), bf16[4,256,768]{2,1,0:T(8,128)(2,1)}, u32[]{:S(2)}, u32[]{:S(2)}) async-start(bf16[4,256,768]{2,1,0:T(8,128)(2,1)} %pad_maximum_fusion), calls=%async_computation.12 | async-start | bytes 3145728 | tf_op jit(solution)/shard_map/all_to_all | solution.py:59
  (58 other events, 271.2 us)
Sparse Core Ops, SparseCore 0:
  22.4 26.2 all-gather.5
  102.2 31.7 reduce-scatter.4
  137.5 33.7 all-gather.7
  172.8 33.7 all-gather.9
  235.7 31.4 reduce-scatter.8
  272.1 22.5 all-gather.11
  351.7 259.6 all-reduce.7
  614.5 36.0 reduce-scatter.10
  653.8 40.6 reduce-scatter.6
